TPU v7x, 32 devices: a whole 2x2x4 slice. The times are simulated.
32 devices in a mesh: expert: 8 (over z, y), dp: 4 (over x, core).
Axes of the slice: x: 2, y: 2, z: 4, core: 2. Of those that a mesh axis runs over, the one named last changes fastest.
Arguments:
- tokens: bfloat16 [4096, 3584], P(('expert', 'dp')), may hold values from -6 to 6
- cotangent: bfloat16 [4096, 3584], P(('expert', 'dp')), may hold values from -6 to 6
- routes: int32 [4096, 1], P(('expert', 'dp')), may hold values from 0 to 1; in each aligned block of 128 rows (0 to 127, 128 to 255, ...) at most 80 rows name the same one
- gates: bfloat16 [4096, 1], P(('expert', 'dp')), may hold values from 0.049804688 to 1
- w_gate: bfloat16 [2048, 3584], P('expert', 'dp'), may hold values from -0.09375 to 0.09375
- w_up: bfloat16 [2048, 3584], P('expert', 'dp'), may hold values from -0.09375 to 0.09375
- w_down: bfloat16 [2048, 3584], P('expert', 'dp'), may hold values from -0.1875 to 0.1875
Outputs:
- grad_up: bfloat16 [2048, 3584], P('expert', 'dp')
- grad_down: bfloat16 [2048, 3584], P('expert', 'dp')
- grad_gates: float32 [4096, 1], P(('expert', 'dp'))
Inputs may be any that keep to these rules, and one draw needn't show every extreme that they name: `routes`: the 1 entries of a row are distinct. Among the 128 rows of one device, no expert is named more than 80 times, a bound that some block reaches.
All inputs are finite; a program needn't handle non-finite values.
Results may differ from a plain program's by a relative error of at most 0.009.
Values may be sent and summed in bfloat16 or wider, within the bound.
A program may use at most 128 MiB of HBM per device.

v0:
```python
import jax
import jax.numpy as jnp
from jax import lax
from jax.experimental import pallas as pl
from jax.experimental.pallas import tpu as pltpu
from jax.sharding import PartitionSpec as P

SPLIT = 4
TOP = 1
TOK_DEV = 128
MESH = pl.DeviceIdType.MESH
PIECES = 4
ORDER = (0, 4, 1, 5)
PLACE = {c: i for i, c in enumerate(ORDER)}


def flip(index, code):
    for bit in (1, 2, 4):
        if code & bit:
            index = index + bit - 2 * bit * ((index // bit) % 2)
    return index


def fused_kernel(
    cap, oh_ref, ohg_ref, tok_ref, cot_ref, wg_ref, wu_ref, wd_ref,
    up_ref, down_ref, share_ref,
    rows_x, rows_c, far_x, far_c, w_all, t_a, t_b, t_p, t_h, t_d,
    part, from_core, to_first, from_first, to_second, from_second, share_mine, share_all,
    local_sem, row_send, row_recv, w_send, w_recv, core_send, core_recv,
    first_send, first_recv, second_send, second_recv, share_send, share_recv,
):
    e = lax.axis_index("expert")
    d = lax.axis_index("dp")
    hidden, cols = wg_ref.shape
    nt = (((1,), (1,)), ((), ()))
    nn = (((1,), (0,)), ((), ()))
    f32, bf16 = jnp.float32, jnp.bfloat16
    to_y, to_z = {"expert": flip(e, 1)}, {"expert": flip(e, 2)}
    to_core_dev, to_x = {"dp": flip(d, 1)}, {"dp": flip(d, 2)}

    barrier = pltpu.get_barrier_semaphore()
    for code in (1, 2, 4, 5):
        pl.semaphore_signal(barrier, inc=1, device_id={"expert": flip(e, code)}, device_id_type=MESH)
    for code in (1, 2):
        pl.semaphore_signal(barrier, inc=1, device_id={"dp": flip(d, code)}, device_id_type=MESH)
    pl.semaphore_wait(barrier, 6)

    sent = []

    def push(src, dst, send_sem, recv_sem, device):
        copy = pltpu.make_async_remote_copy(
            src_ref=src, dst_ref=dst, send_sem=send_sem, recv_sem=recv_sem,
            device_id=device, device_id_type=MESH,
        )
        copy.start()
        sent.append(copy)
        return copy

    def band(index):
        return pl.ds(pl.multiple_of(index * cols, 128), cols)

    w_in = (wg_ref, wu_ref, wd_ref)
    w_copy = {}

    def w_at(k, part_of, code):
        return w_all.at[k, part_of * hidden : (part_of + 1) * hidden, band(flip(d, code))]

    def w_push(k, source, code, device, there, there_code):
        number = there * 4 + there_code
        w_copy[k, there, there_code] = push(
            source, w_all.at[k, there * hidden : (there + 1) * hidden, band(flip(d, code))],
            w_send.at[k, number], w_recv.at[k, number], device,
        )

    local = []

    def w_own(k):
        w_push(k, w_in[k], 0, to_z, 1, 0)
        w_push(k, w_in[k], 0, to_x, 0, 2)
        w_push(k, w_in[k], 0, to_core_dev, 0, 1)
        here = pltpu.make_async_copy(w_in[k], w_at(k, 0, 0), local_sem.at[k])
        here.start()
        local.append(here)

    def w_first(k):
        w_copy[k, 1, 0].wait_recv()
        w_push(k, w_at(k, 1, 0), 0, to_x, 1, 2)
        w_push(k, w_at(k, 1, 0), 0, to_core_dev, 1, 1)
        w_copy[k, 0, 2].wait_recv()
        w_push(k, w_at(k, 0, 2), 2, to_core_dev, 0, 3)

    def w_last(k):
        w_copy[k, 1, 2].wait_recv()
        w_push(k, w_at(k, 1, 2), 2, to_core_dev, 1, 3)

    def w_ready(k):
        local[k].wait()
        for key in ((0, 1), (1, 1), (0, 3), (1, 3)):
            w_copy[(k,) + key].wait_recv()

    step = rows_x.shape[1] // PIECES

    def at(ref, code, piece):
        return ref.at[pl.ds(PLACE[code] * cap, cap), pl.ds(piece * step, step)]

    rows = (rows_x, rows_c)
    row_copy = {}

    def send_row(kind, slot, hop, piece, source=None):
        there = slot ^ hop
        row_copy[kind, there, piece] = push(
            at(rows[kind], slot, piece) if source is None else source, at(rows[kind], there, piece),
            row_send.at[kind, there, piece], row_recv.at[kind, there, piece], {"expert": flip(e, hop)},
        )

    def got(kind, code, piece):
        row_copy[kind, code, piece].wait_recv()

    def got_all(kind, code):
        for piece in range(PIECES):
            got(kind, code, piece)

    hots = (oh_ref, ohg_ref)
    whole = (tok_ref, cot_ref)
    fars = (far_x, far_c)

    def pick(kind, low, piece):
        return lax.dot_general(
            hots[kind][low : low + cap, :], whole[kind][:, piece * step : (piece + 1) * step], nn,
            preferred_element_type=f32,
        ).astype(bf16)

    def send_far(kind, piece):
        lanes = pl.ds(piece * step, step)
        fars[kind][:, lanes] = pick(kind, cap, piece)
        send_row(kind, 0, 4, piece, fars[kind].at[:, lanes])

    def send_near(kind, piece):
        at(rows[kind], 0, piece)[...] = pick(kind, 0, piece)
        send_row(kind, 0, 1, piece)

    def pass_on(kind, piece):
        got(kind, 4, piece)
        send_row(kind, 4, 1, piece)

    send_far(0, 0)
    send_near(0, 0)
    send_far(0, 1)
    w_own(0)
    send_near(0, 1)
    send_far(0, 2)
    send_near(0, 2)
    send_far(0, 3)
    send_near(0, 3)
    w_own(1)
    send_far(1, 0)
    send_near(1, 0)
    send_far(1, 1)
    send_near(1, 1)
    w_own(2)
    send_far(1, 2)
    send_near(1, 2)
    send_far(1, 3)
    send_near(1, 3)

    def project(dst, k, kind):
        for i in range(2):
            dst[i * hidden : (i + 1) * hidden, :] = lax.dot_general(
                w_all[k, i * hidden : (i + 1) * hidden, :], rows[kind][...], nt, preferred_element_type=f32
            )

    left = (t_d, t_h)
    right = (rows_x, rows_c)

    def block(g, i, code):
        part[g, i, code] = lax.dot_general(
            left[g][i * hidden : (i + 1) * hidden, :], right[g][:, band(flip(d, code))], nn,
            preferred_element_type=f32,
        ).astype(bf16)

    core_copy = {}
    first_copy = {}
    second_copy = {}

    def to_core(g, i, code):
        block(g, i, code)
        n = code // 2
        core_copy[g, i, n] = push(
            part.at[g, i, code], from_core.at[g, i, n],
            core_send.at[g, i * 2 + n], core_recv.at[g, i * 2 + n], to_core_dev,
        )

    def both(g, i, n):
        core_copy[g, i, n].wait_recv()
        return part[g, i, 2 * n].astype(f32) + from_core[g, i, n].astype(f32)

    def first(g, i, n, number, device):
        to_first[g, number] = both(g, i, n).astype(bf16)
        first_copy[g, number] = push(
            to_first.at[g, number], from_first.at[g, number],
            first_send.at[g, number], first_recv.at[g, number], device,
        )

    def second(g, i, n, device):
        mine = both(g, i, n)
        first_copy[g, 1].wait_recv()
        to_second[g] = (mine + from_first[g, 1].astype(f32)).astype(bf16)
        second_copy[g] = push(
            to_second.at[g], from_second.at[g], second_send.at[g], second_recv.at[g], device
        )

    pass_on(0, 0)
    pass_on(0, 1)
    w_first(0)
    pass_on(0, 2)
    pass_on(0, 3)
    w_first(1)
    pass_on(1, 0)
    pass_on(1, 1)
    w_last(0)
    w_first(2)
    pass_on(1, 2)
    pass_on(1, 3)
    w_last(1)
    got_all(0, 1)
    got_all(0, 5)
    w_ready(0)
    project(t_a, 0, 0)
    w_ready(1)
    project(t_b, 1, 0)
    a = t_a[...]
    silu = a * jax.nn.sigmoid(a)
    t_h[...] = (silu * t_b[...]).astype(bf16)
    t_a[...] = silu
    got_all(1, 1)
    got_all(1, 5)

    to_core(1, 1, 3)
    to_core(1, 1, 1)
    block(1, 1, 2)
    block(1, 1, 0)
    first(1, 1, 1, 1, to_z)
    first(1, 1, 0, 0, to_z)
    w_last(2)
    to_core(1, 0, 3)
    to_core(1, 0, 1)
    block(1, 0, 2)
    block(1, 0, 0)
    w_ready(2)
    project(t_p, 2, 1)
    p = t_p[...]
    t_d[...] = (p * t_a[...]).astype(bf16)

    to_core(0, 1, 3)
    to_core(0, 0, 3)
    block(0, 1, 2)
    block(0, 0, 2)
    first(0, 1, 1, 1, to_x)
    second(1, 0, 1, to_x)
    first(0, 0, 1, 0, to_x)
    to_core(0, 1, 1)
    to_core(0, 0, 1)
    block(0, 1, 0)
    block(0, 0, 0)

    total = jnp.sum(t_h[...].astype(f32) * t_p[...], axis=0, keepdims=True)
    share_mine[...] = jnp.broadcast_to(total, share_mine.shape)
    share_copy = {}
    for code in (1, 4, 5):
        n = PLACE[code]
        share_copy[n] = push(
            share_mine, share_all.at[n], share_send.at[n], share_recv.at[n], {"expert": flip(e, code)}
        )
    second(0, 1, 0, to_z)
    share_ref[0:1, :] = share_mine[0:1, :]
    for n in (1, 2, 3):
        share_copy[n].wait_recv()
        share_ref[n : n + 1, :] = share_all[n, 0:1, :]
    for g, out in ((1, down_ref), (0, up_ref)):
        core_copy[g, 0, 0].wait_recv()
        mine = part[g, 0, 0].astype(f32) + from_core[g, 0, 0].astype(f32)
        first_copy[g, 0].wait_recv()
        mine = mine + from_first[g, 0].astype(f32)
        second_copy[g].wait_recv()
        out[...] = (mine + from_second[g].astype(f32)).astype(bf16)
    for copy in sent:
        copy.wait_send()


def fused(cap, tokens, cotangent, routes, gates, w_gate, w_up, w_down):
    near = lax.axis_index("expert") // SPLIT
    flat, slot = slot_of(routes, 2)
    ids = jnp.arange(2 * cap, dtype=jnp.int32)
    named = jnp.where(ids < cap, near, 1 - near)
    placed = (flat[None, :] == named[:, None]) & (slot[None, :] == (ids % cap)[:, None])
    hot = placed.astype(jnp.bfloat16)
    weight = gates.reshape(-1)
    hot_gate = jnp.where(placed, weight[None, :], jnp.zeros((), jnp.bfloat16))
    width = tokens.shape[1]
    hidden, cols = w_gate.shape
    count = len(ORDER) * cap
    bf16, f32 = jnp.bfloat16, jnp.float32
    vmem = pl.BlockSpec(memory_space=pltpu.VMEM)
    anywhere = pl.BlockSpec(memory_space=pl.ANY)
    dma = pltpu.SemaphoreType.DMA
    up, down, share = pl.pallas_call(
        lambda *refs: fused_kernel(cap, *refs),
        out_shape=(
            jax.ShapeDtypeStruct((hidden, cols), bf16),
            jax.ShapeDtypeStruct((hidden, cols), bf16),
            jax.ShapeDtypeStruct((4, count), f32),
        ),
        in_specs=[vmem] * 4 + [anywhere] * 3,
        out_specs=(vmem, vmem, vmem),
        scratch_shapes=[
            pltpu.VMEM((count, width), bf16),
            pltpu.VMEM((count, width), bf16),
            pltpu.VMEM((cap, width), bf16),
            pltpu.VMEM((cap, width), bf16),
            pltpu.VMEM((3, 2 * hidden, width), bf16),
            pltpu.VMEM((2 * hidden, count), f32),
            pltpu.VMEM((2 * hidden, count), f32),
            pltpu.VMEM((2 * hidden, count), f32),
            pltpu.VMEM((2 * hidden, count), bf16),
            pltpu.VMEM((2 * hidden, count), bf16),
            pltpu.VMEM((2, 2, 4, hidden, cols), bf16),
            pltpu.VMEM((2, 2, 2, hidden, cols), bf16),
            pltpu.VMEM((2, 2, hidden, cols), bf16),
            pltpu.VMEM((2, 2, hidden, cols), bf16),
            pltpu.VMEM((2, hidden, cols), bf16),
            pltpu.VMEM((2, hidden, cols), bf16),
            pltpu.VMEM((8, count), f32),
            pltpu.VMEM((4, 8, count), f32),
            dma((3,)),
            dma((2, 8, PIECES)), dma((2, 8, PIECES)),
            dma((3, 8)), dma((3, 8)),
            dma((2, 4)), dma((2, 4)),
            dma((2, 2)), dma((2, 2)),
            dma((2,)), dma((2,)),
            dma((4,)), dma((4,)),
        ],
        compiler_params=pltpu.CompilerParams(
            collective_id=0, has_side_effects=True, vmem_limit_bytes=60 * 1024 * 1024
        ),
    )(hot, hot_gate, tokens, cotangent, w_gate, w_up, w_down)
    sums = []
    for codes in ((0, 1), (4, 5)):
        sums.append(sum(share[PLACE[c], PLACE[c] * cap : (PLACE[c] + 1) * cap] for c in codes))
    summed = jnp.concatenate(sums)
    gate_grad = jnp.sum(jnp.where(placed, summed[:, None], 0.0), axis=0)
    gate_grad = gate_grad / weight.astype(f32)
    return up, down, gate_grad.reshape(tokens.shape[0], TOP)


def partner(array, axis, bit):
    return lax.ppermute(array, axis, [(i, i ^ 1 << bit) for i in range(lax.axis_size(axis))])


def slot_of(routes, experts):
    flat = routes.reshape(-1)
    owner = (flat[:, None] == jnp.arange(experts, dtype=jnp.int32)[None, :]).astype(jnp.int32)
    before = jnp.cumsum(owner, axis=0) - owner
    slot = jnp.sum(before * owner, axis=1)
    return (flat, slot)


def shards(tokens, cotangent, routes, gates, w_gate, w_up, w_down):
    tok_count = tokens.shape[0]
    groups = lax.axis_size("expert")
    experts = groups // SPLIT
    capacity = max(2, min(TOK_DEV, 5 * TOK_DEV * TOP // (4 * experts)))
    if groups == 8 and lax.axis_size("dp") == 4 and capacity % 16 == 0 and capacity > 64:
        return fused(capacity, tokens, cotangent, routes, gates, w_gate, w_up, w_down)
    piece = (capacity + SPLIT - 1) // SPLIT
    levels = SPLIT.bit_length() - 1
    here = lax.axis_index("expert")
    flat, slot = slot_of(routes, experts)
    pair_count = flat.shape[0]
    pair_tok = (
        (jnp.arange(pair_count, dtype=jnp.int32) // TOP)[:, None]
        == jnp.arange(tok_count, dtype=jnp.int32)[None, :]
    ).astype(jnp.bfloat16)
    rows_all = groups * piece
    row_ids = jnp.arange(rows_all, dtype=jnp.int32)
    dest = row_ids // piece
    row_expert = dest // SPLIT
    row_slot = dest % SPLIT + row_ids % piece * SPLIT
    placed = (flat[None, :] == row_expert[:, None]) & (slot[None, :] == row_slot[:, None])
    placed_f = placed.astype(jnp.float32)
    token_map = jnp.dot(
        placed.astype(jnp.bfloat16), pair_tok, preferred_element_type=jnp.float32
    ).astype(jnp.bfloat16)
    send_x = jnp.dot(token_map, tokens, preferred_element_type=jnp.float32).astype(jnp.bfloat16)
    send_dy = jnp.dot(token_map, cotangent, preferred_element_type=jnp.float32).astype(jnp.bfloat16)
    send_gate = jnp.dot(
        placed_f, gates.reshape(-1).astype(jnp.float32), precision=lax.Precision.HIGHEST
    ).astype(jnp.bfloat16)
    full_gate, full_up, full_down = (
        lax.all_gather(w_gate, "dp", axis=1, tiled=True),
        lax.all_gather(w_up, "dp", axis=1, tiled=True),
        lax.all_gather(w_down, "dp", axis=1, tiled=True),
    )
    cur_x, cur_dy, cur_g = (
        lax.all_to_all(send_x, "expert", split_axis=0, concat_axis=0, tiled=True),
        lax.all_to_all(send_dy, "expert", split_axis=0, concat_axis=0, tiled=True),
        lax.all_to_all(send_gate, "expert", split_axis=0, concat_axis=0, tiled=True),
    )
    for bit in range(levels):
        got = partner((cur_x, cur_dy, cur_g), "expert", bit)
        lower = here // (1 << bit) % 2 == 0
        cur_x = jnp.where(
            lower,
            jnp.concatenate([cur_x, got[0]], axis=0),
            jnp.concatenate([got[0], cur_x], axis=0),
        )
        cur_dy = jnp.where(
            lower,
            jnp.concatenate([cur_dy, got[1]], axis=0),
            jnp.concatenate([got[1], cur_dy], axis=0),
        )
        cur_g = jnp.where(
            lower,
            jnp.concatenate([cur_g, got[2]], axis=0),
            jnp.concatenate([got[2], cur_g], axis=0),
        )
    rows_x, rows_dy, recv_gate = (cur_x, cur_dy, cur_g)
    pre_a = lax.dot_general(
        rows_x, full_gate, (((1,), (1,)), ((), ())), preferred_element_type=jnp.float32
    )
    pre_b = lax.dot_general(
        rows_x, full_up, (((1,), (1,)), ((), ())), preferred_element_type=jnp.float32
    )
    sig = jax.nn.sigmoid(pre_a)
    silu = pre_a * sig
    hidden = (silu * pre_b).astype(jnp.bfloat16)
    weight = recv_gate.astype(jnp.float32)
    probe = lax.dot_general(
        rows_dy, full_down, (((1,), (1,)), ((), ())), preferred_element_type=jnp.float32
    )
    share = jnp.sum(hidden.astype(jnp.float32) * probe, axis=1)
    scaled = (weight[:, None] * rows_dy.astype(jnp.float32)).astype(jnp.bfloat16)
    d_b = (weight[:, None] * probe * silu).astype(jnp.bfloat16)
    part_up = lax.dot_general(
        d_b, rows_x, (((0,), (0,)), ((), ())), preferred_element_type=jnp.float32
    )
    part_down = lax.dot_general(
        hidden, scaled, (((0,), (0,)), ((), ())), preferred_element_type=jnp.float32
    )
    folded = share.reshape(SPLIT, rows_all)
    for bit in reversed(range(levels)):
        half = folded.shape[0] // 2
        lower_half = folded[:half]
        upper_half = folded[half:]
        lower = here // (1 << bit) % 2 == 0
        keep = jnp.where(lower, lower_half, upper_half)
        away = jnp.where(lower, upper_half, lower_half)
        folded = keep + partner(away, "expert", bit)
    summed = lax.all_to_all(
        folded.reshape(rows_all), "expert", split_axis=0, concat_axis=0, tiled=True
    )
    gate_grad = jnp.dot(placed_f.T, summed, precision=lax.Precision.HIGHEST)
    sum_up, sum_down = (
        lax.psum_scatter(
            part_up.astype(jnp.bfloat16), "dp", scatter_dimension=1, tiled=True
        ).astype(jnp.float32),
        lax.psum_scatter(
            part_down.astype(jnp.bfloat16), "dp", scatter_dimension=1, tiled=True
        ).astype(jnp.float32),
    )
    return (
        sum_up.astype(jnp.bfloat16),
        sum_down.astype(jnp.bfloat16),
        gate_grad.reshape(tok_count, TOP),
    )


def solution(mesh):
    in_specs = (
        P(("expert", "dp"), None),
        P(("expert", "dp"), None),
        P(("expert", "dp"), None),
        P(("expert", "dp"), None),
        P("expert", "dp"),
        P("expert", "dp"),
        P("expert", "dp"),
    )
    out_specs = (P("expert", "dp"), P("expert", "dp"), P(("expert", "dp"), None))
    return jax.shard_map(shards, mesh=mesh, in_specs=in_specs, out_specs=out_specs, check_vma=False)
```

profile of v0, /device:TPU:0, one launch (start us, length us, event | category | flops | bytes accessed | tf_op | source)
XLA Modules:
  0.0 121.5 jit_solution(2504906904218636843)
XLA Ops:
  0.7 0.0 copy-start.1
  0.7 0.6 copy-done.1
  1.3 0.1 fusion
  1.4 0.2 reduce_window_sum.11
  1.6 0.2 select_reduce_fusion.1
  1.8 0.0 copy-start.2
  1.8 0.7 copy-done.2
  2.4 0.7 fusion.1.refs_1_
  3.1 0.7 fusion.2.refs_0_
  3.9 113.4 %shard_map.94 = (bf16[256,896]{1,0:T(8,128)(2,1)}, bf16[256,896]{1,0:T(8,128)(2,1)}, f32[4,320]{1,0:T(4,128)}) custom-call(bf16[160,128]{1,0:T(8,128)(2,1)} %fusion.2.refs_0_, bf16[160,128]{1,0:T(8,128)(2,1)} %fusion.1.refs_1_, bf16[128,3584]{1,0:T(8,128)(2,1)} %refs_2_.1, bf16[128,3584]{1,0:T(8,128)(2,1)} %refs_3_.1, bf16[256,896]{1,0:T(8,128)(2,1)} %refs_4_.1, ...), custom_call_target="tpu_custom_call" | custom-call | tf_op jit(solution)/shard_map/pallas_call | solution.py:306
  117.3 0.9 add_bitcast_fusion.1
  118.1 0.1 pad_maximum_fusion
  118.2 0.1 select_reduce_fusion
  118.4 0.5 bitcast_divide_fusion
  118.9 0.0 copy-start
  118.9 1.9 %copy.12 = bf16[256,896]{1,0:T(8,128)(2,1)} copy(bf16[256,896]{1,0:T(8,128)(2,1)} %get-tuple-element.16) | data formatting | bytes 917504
  120.8 0.0 copy-done
  120.8 0.8 copy.13
  (1 shorter events, 0.0 us)
Async XLA Ops:
  0.7 0.7 copy-start.1
  1.8 0.7 copy-start.2
  118.9 1.9 %copy-start = (bf16[256,896]{1,0:T(8,128)(2,1)S(1)}, bf16[256,896]{1,0:T(8,128)(2,1)}, u32[]{:S(2)}) copy-start(bf16[256,896]{1,0:T(8,128)(2,1)} %get-tuple-element.17) | copy-start | bytes 1376260
where the time goes:
time: 122 us
  Pallas kernels  113 us (93%)
  local copies, waits for them, and re-layouts  3.95 us (3%)
  other arithmetic  3.5 us (3%)
    pallas_call x1, Pallas kernels, fused(): pl.pallas_call(lambda *refs: fused_kernel(cap, *refs), out_shape=(jax.Sha...  113 us
    unnamed x8, local copies, waits for them, and re-layouts  3.95 us

commit v1 on v0

v1 whole, which is shorter than its diff:
```python
import jax
import jax.numpy as jnp
from jax import lax
from jax.experimental import pallas as pl
from jax.experimental.pallas import tpu as pltpu
from jax.sharding import PartitionSpec as P

SPLIT = 4
TOP = 1
TOK_DEV = 128
MESH = pl.DeviceIdType.MESH
ORDER = (0, 4, 1, 5)
PLACE = {c: i for i, c in enumerate(ORDER)}
PIECE = 256


def flip(index, code):
    for bit in (1, 2, 4):
        if code & bit:
            index = index + bit - 2 * bit * ((index // bit) % 2)
    return index


def fused_kernel(
    cap, oh_ref, ohg_ref, tok_ref, cot_ref, wg_ref, wu_ref, wd_ref,
    up_ref, down_ref, share_ref,
    rows_x, rows_c, near, far, w_all, t_sum, core_out, core_in, x_out, x_in, t_h, t_d,
    own, z_out, z_in, share_mine, share_all,
    local_sem, row_send, row_recv, w_send, w_recv, core_send, core_recv, x_send, x_recv,
    act_send, act_recv, z_send, z_recv, share_send, share_recv,
):
    e = lax.axis_index("expert")
    d = lax.axis_index("dp")
    hidden, cols = wg_ref.shape
    half = t_sum.shape[2]
    per = hidden // PIECE
    nt = (((1,), (1,)), ((), ()))
    nn = (((1,), (0,)), ((), ()))
    f32, bf16 = jnp.float32, jnp.bfloat16
    x_here = d // 2
    x_there = 1 - x_here

    def at_device(code, rel):
        return {"expert": flip(e, code), "dp": flip(d, rel)}

    barrier = pltpu.get_barrier_semaphore()
    peers = ((0, 1), (0, 2), (0, 3), (1, 0), (2, 0), (4, 0), (4, 1), (4, 2), (4, 3), (5, 0))
    for code, rel in peers:
        pl.semaphore_signal(barrier, inc=1, device_id=at_device(code, rel), device_id_type=MESH)
    pl.semaphore_wait(barrier, len(peers))

    sent = []

    def push(src, dst, send_sem, recv_sem, device):
        copy = pltpu.make_async_remote_copy(
            src_ref=src, dst_ref=dst, send_sem=send_sem, recv_sem=recv_sem,
            device_id=device, device_id_type=MESH,
        )
        copy.start()
        sent.append(copy)
        return copy

    rows = (rows_x, rows_c)
    whole = (tok_ref, cot_ref)
    hots = (oh_ref, ohg_ref)

    def block(kind, rel, source_x, code):
        number = (rel % 2) * 8 + source_x * 4 + PLACE[code]
        return rows[kind].at[pl.ds(pl.multiple_of(number * cap, 16), cap), :]

    def pick(kind, low, rel):
        lanes = pl.ds(pl.multiple_of(flip(d, rel) * cols, 128), cols)
        return lax.dot_general(
            hots[kind][low : low + cap, :], whole[kind][:, lanes], nn, preferred_element_type=f32
        ).astype(bf16)

    row_copy = {}

    def send_block(kind, code, rel, source, there, source_x, device):
        row_copy[kind, code, rel] = push(
            source, there, row_send.at[kind, PLACE[code], rel], row_recv.at[kind, PLACE[code], rel], device
        )

    def send_far(kind, rel):
        far[kind, rel] = pick(kind, cap, rel)
        send_block(kind, 4, rel, far.at[kind, rel], block(kind, rel, x_here, 4), x_here, at_device(4, rel))

    def send_near(kind, rel):
        if rel == 0:
            mine = block(kind, 0, x_here, 0)
            mine[...] = pick(kind, 0, 0)
            pass_on(kind, 0, 0)
        else:
            near[kind, rel - 1] = pick(kind, 0, rel)
            send_block(
                kind, 0, rel, near.at[kind, rel - 1], block(kind, rel, x_here, 0), x_here, at_device(0, rel)
            )

    def pass_on(kind, code, rel):
        source_x = x_there if rel // 2 else x_here
        send_block(
            kind, code + 1, rel, block(kind, rel, source_x, code), block(kind, rel, source_x, code + 1),
            source_x, at_device(1, 0),
        )

    def got(kind, code, rel):
        row_copy[kind, code, rel].wait_recv()

    def forward(kind, code, rel):
        got(kind, code, rel)
        pass_on(kind, code, rel)

    w_in = (wg_ref, wu_ref, wd_ref)
    w_copy = {}
    local = {}

    def w_own(k):
        w_copy[k] = push(
            w_in[k], w_all.at[k, hidden : 2 * hidden], w_send.at[k], w_recv.at[k], at_device(2, 0)
        )

    def w_keep(k):
        local[k] = pltpu.make_async_copy(w_in[k], w_all.at[k, 0:hidden], local_sem.at[k])
        local[k].start()

    def span(q):
        return slice(q * PIECE, (q + 1) * PIECE)

    core_copy = {}
    x_copy = {}
    act_copy = {}
    z_copy = {}

    def project(k, q):
        out = lax.dot_general(
            w_all[k, span(q), :], rows[k // 2][...], nt, preferred_element_type=f32
        )
        core_out[k, span(q), :] = out[:, half:]
        core_copy[k, q] = push(
            core_out.at[k, span(q)], core_in.at[k, span(q)],
            core_send.at[k, q], core_recv.at[k, q], at_device(0, 1),
        )
        t_sum[k, span(q), :] = out[:, :half]

    def cross(k, q):
        core_copy[k, q].wait_recv()
        both = t_sum[k, span(q), :] + core_in[k, span(q), :]
        x_out[k, span(q), :] = both.astype(bf16)
        x_copy[k, q] = push(
            x_out.at[k, span(q)], x_in.at[k, span(q)], x_send.at[k, q], x_recv.at[k, q], at_device(0, 2)
        )
        t_sum[k, span(q), :] = both

    def total(k, q):
        x_copy[k, q].wait_recv()
        return t_sum[k, span(q), :] + x_in[k, span(q), :].astype(f32)

    def hand_over(g, ref, q):
        act_copy[g, q] = push(
            ref.at[span(q), 0:half], ref.at[span(q), half : 2 * half],
            act_send.at[g, q], act_recv.at[g, q], at_device(0, 1),
        )

    def activate(q):
        a = total(0, q)
        silu = a * jax.nn.sigmoid(a)
        t_h[span(q), 0:half] = (silu * total(1, q)).astype(bf16)
        hand_over(1, t_h, q)
        t_sum[0, span(q), :] = silu

    def derive(q):
        p = total(2, q)
        t_d[span(q), 0:half] = (p * t_sum[0, span(q), :]).astype(bf16)
        hand_over(0, t_d, q)
        t_sum[2, span(q), :] = p

    left = (t_d, t_h)

    def gradient(g, q):
        act_copy[g, q].wait_recv()
        out = lax.dot_general(
            left[g][span(q), :], rows[g][...], nn, preferred_element_type=f32
        )
        if q < per:
            own[g, span(q), :] = out
        else:
            there = span(q - per)
            z_out[g, there, :] = out.astype(bf16)
            z_copy[g, q - per] = push(
                z_out.at[g, there], z_in.at[g, there],
                z_send.at[g, q - per], z_recv.at[g, q - per], at_device(2, 0),
            )

    mine_q = tuple(range(per))
    their_q = tuple(range(per, 2 * per))

    for rel in (2, 0, 3, 1):
        send_far(0, rel)
    for rel in (0, 2, 3, 1):
        send_near(0, rel)
    for k in (0, 1):
        w_own(k)
    for k in (0, 1, 2):
        w_keep(k)
    for rel in (2, 0, 3, 1):
        send_far(1, rel)
    for rel in (2, 3, 1):
        send_near(1, rel)
    w_own(2)
    for rel in (1, 2, 3):
        forward(0, 0, rel)
    for rel in (0, 1, 2, 3):
        forward(0, 4, rel)
    send_near(1, 0)
    for rel in (1, 2, 3):
        forward(1, 0, rel)
    for code in (1, 5):
        for rel in (0, 1, 2, 3):
            got(0, code, rel)
    for k in (0, 1):
        local[k].wait()
        for q in mine_q:
            project(k, q)
    for k in (0, 1):
        for q in mine_q:
            cross(k, q)
    for rel in (0, 1):
        forward(1, 4, rel)
    for k in (0, 1):
        w_copy[k].wait_recv()
        for q in their_q:
            project(k, q)
    for k in (0, 1):
        for q in their_q:
            cross(k, q)
    for rel in (2, 3):
        forward(1, 4, rel)
    for q in mine_q:
        activate(q)
    for code in (1, 5):
        for rel in (0, 1, 2, 3):
            got(1, code, rel)
    w_copy[2].wait_recv()
    for q in their_q:
        project(2, q)
    local[2].wait()
    for q in their_q:
        cross(2, q)
    for q in mine_q:
        project(2, q)
    for q in mine_q:
        cross(2, q)
    for q in their_q:
        activate(q)
    for q in their_q:
        gradient(1, q)
    for q in mine_q:
        gradient(1, q)
    for q in their_q:
        derive(q)
        gradient(0, q)
    for q in mine_q:
        derive(q)
    dots = jnp.sum(t_h[:, 0:half].astype(f32) * t_sum[2], axis=0, keepdims=True)
    share_mine[...] = jnp.broadcast_to(dots, share_mine.shape)
    share_copy = {}
    for code in (1, 4, 5):
        n = PLACE[code]
        share_copy[n] = push(
            share_mine, share_all.at[n], share_send.at[n], share_recv.at[n], at_device(code, 0)
        )
    share_ref[0:1, :] = share_mine[0:1, :]
    for q in mine_q:
        gradient(0, q)
    for g, out in ((1, down_ref), (0, up_ref)):
        for q in mine_q:
            z_copy[g, q].wait_recv()
            out[span(q), :] = (own[g, span(q), :] + z_in[g, span(q), :].astype(f32)).astype(bf16)
    for n in (1, 2, 3):
        share_copy[n].wait_recv()
        share_ref[n : n + 1, :] = share_all[n, 0:1, :]
    for copy in sent:
        copy.wait_send()


def fused(cap, tokens, cotangent, routes, gates, w_gate, w_up, w_down):
    near = lax.axis_index("expert") // SPLIT
    flat, slot = slot_of(routes, 2)
    ids = jnp.arange(2 * cap, dtype=jnp.int32)
    named = jnp.where(ids < cap, near, 1 - near)
    placed = (flat[None, :] == named[:, None]) & (slot[None, :] == (ids % cap)[:, None])
    hot = placed.astype(jnp.bfloat16)
    weight = gates.reshape(-1)
    hot_gate = jnp.where(placed, weight[None, :], jnp.zeros((), jnp.bfloat16))
    hidden, cols = w_gate.shape
    half = 8 * cap
    per = hidden // PIECE
    bf16, f32 = jnp.bfloat16, jnp.float32
    vmem = pl.BlockSpec(memory_space=pltpu.VMEM)
    anywhere = pl.BlockSpec(memory_space=pl.ANY)
    dma = pltpu.SemaphoreType.DMA
    up, down, share = pl.pallas_call(
        lambda *refs: fused_kernel(cap, *refs),
        out_shape=(
            jax.ShapeDtypeStruct((hidden, cols), bf16),
            jax.ShapeDtypeStruct((hidden, cols), bf16),
            jax.ShapeDtypeStruct((4, half), f32),
        ),
        in_specs=[vmem] * 4 + [anywhere] * 3,
        out_specs=(vmem, vmem, vmem),
        scratch_shapes=[
            pltpu.VMEM((2 * half, cols), bf16),
            pltpu.VMEM((2 * half, cols), bf16),
            pltpu.VMEM((2, 3, cap, cols), bf16),
            pltpu.VMEM((2, 4, cap, cols), bf16),
            pltpu.VMEM((3, 2 * hidden, cols), bf16),
            pltpu.VMEM((3, 2 * hidden, half), f32),
            pltpu.VMEM((3, 2 * hidden, half), f32),
            pltpu.VMEM((3, 2 * hidden, half), f32),
            pltpu.VMEM((3, 2 * hidden, half), bf16),
            pltpu.VMEM((3, 2 * hidden, half), bf16),
            pltpu.VMEM((2 * hidden, 2 * half), bf16),
            pltpu.VMEM((2 * hidden, 2 * half), bf16),
            pltpu.VMEM((2, hidden, cols), f32),
            pltpu.VMEM((2, hidden, cols), bf16),
            pltpu.VMEM((2, hidden, cols), bf16),
            pltpu.VMEM((8, half), f32),
            pltpu.VMEM((4, 8, half), f32),
            dma((3,)),
            dma((2, 4, 4)), dma((2, 4, 4)),
            dma((3,)), dma((3,)),
            dma((3, 2 * per)), dma((3, 2 * per)),
            dma((3, 2 * per)), dma((3, 2 * per)),
            dma((2, 2 * per)), dma((2, 2 * per)),
            dma((2, per)), dma((2, per)),
            dma((4,)), dma((4,)),
        ],
        compiler_params=pltpu.CompilerParams(
            collective_id=0, has_side_effects=True, vmem_limit_bytes=60 * 1024 * 1024
        ),
    )(hot, hot_gate, tokens, cotangent, w_gate, w_up, w_down)
    count = len(ORDER) * cap
    share = lax.dynamic_slice_in_dim(share, lax.axis_index("dp") // 2 * count, count, 1)
    sums = []
    for codes in ((0, 1), (4, 5)):
        sums.append(sum(share[PLACE[c], PLACE[c] * cap : (PLACE[c] + 1) * cap] for c in codes))
    summed = jnp.concatenate(sums)
    gate_grad = jnp.sum(jnp.where(placed, summed[:, None], 0.0), axis=0)
    gate_grad = gate_grad / weight.astype(f32)
    return up, down, gate_grad.reshape(tokens.shape[0], TOP)


def partner(array, axis, bit):
    return lax.ppermute(array, axis, [(i, i ^ 1 << bit) for i in range(lax.axis_size(axis))])


def slot_of(routes, experts):
    flat = routes.reshape(-1)
    owner = (flat[:, None] == jnp.arange(experts, dtype=jnp.int32)[None, :]).astype(jnp.int32)
    before = jnp.cumsum(owner, axis=0) - owner
    slot = jnp.sum(before * owner, axis=1)
    return (flat, slot)


def shards(tokens, cotangent, routes, gates, w_gate, w_up, w_down):
    tok_count = tokens.shape[0]
    groups = lax.axis_size("expert")
    experts = groups // SPLIT
    capacity = max(2, min(TOK_DEV, 5 * TOK_DEV * TOP // (4 * experts)))
    if groups == 8 and lax.axis_size("dp") == 4 and capacity % 16 == 0 and capacity > 64 and w_gate.shape[0] % PIECE == 0:
        return fused(capacity, tokens, cotangent, routes, gates, w_gate, w_up, w_down)
    piece = (capacity + SPLIT - 1) // SPLIT
    levels = SPLIT.bit_length() - 1
    here = lax.axis_index("expert")
    flat, slot = slot_of(routes, experts)
    pair_count = flat.shape[0]
    pair_tok = (
        (jnp.arange(pair_count, dtype=jnp.int32) // TOP)[:, None]
        == jnp.arange(tok_count, dtype=jnp.int32)[None, :]
    ).astype(jnp.bfloat16)
    rows_all = groups * piece
    row_ids = jnp.arange(rows_all, dtype=jnp.int32)
    dest = row_ids // piece
    row_expert = dest // SPLIT
    row_slot = dest % SPLIT + row_ids % piece * SPLIT
    placed = (flat[None, :] == row_expert[:, None]) & (slot[None, :] == row_slot[:, None])
    placed_f = placed.astype(jnp.float32)
    token_map = jnp.dot(
        placed.astype(jnp.bfloat16), pair_tok, preferred_element_type=jnp.float32
    ).astype(jnp.bfloat16)
    send_x = jnp.dot(token_map, tokens, preferred_element_type=jnp.float32).astype(jnp.bfloat16)
    send_dy = jnp.dot(token_map, cotangent, preferred_element_type=jnp.float32).astype(jnp.bfloat16)
    send_gate = jnp.dot(
        placed_f, gates.reshape(-1).astype(jnp.float32), precision=lax.Precision.HIGHEST
    ).astype(jnp.bfloat16)
    full_gate, full_up, full_down = (
        lax.all_gather(w_gate, "dp", axis=1, tiled=True),
        lax.all_gather(w_up, "dp", axis=1, tiled=True),
        lax.all_gather(w_down, "dp", axis=1, tiled=True),
    )
    cur_x, cur_dy, cur_g = (
        lax.all_to_all(send_x, "expert", split_axis=0, concat_axis=0, tiled=True),
        lax.all_to_all(send_dy, "expert", split_axis=0, concat_axis=0, tiled=True),
        lax.all_to_all(send_gate, "expert", split_axis=0, concat_axis=0, tiled=True),
    )
    for bit in range(levels):
        got = partner((cur_x, cur_dy, cur_g), "expert", bit)
        lower = here // (1 << bit) % 2 == 0
        cur_x = jnp.where(
            lower,
            jnp.concatenate([cur_x, got[0]], axis=0),
            jnp.concatenate([got[0], cur_x], axis=0),
        )
        cur_dy = jnp.where(
            lower,
            jnp.concatenate([cur_dy, got[1]], axis=0),
            jnp.concatenate([got[1], cur_dy], axis=0),
        )
        cur_g = jnp.where(
            lower,
            jnp.concatenate([cur_g, got[2]], axis=0),
            jnp.concatenate([got[2], cur_g], axis=0),
        )
    rows_x, rows_dy, recv_gate = (cur_x, cur_dy, cur_g)
    pre_a = lax.dot_general(
        rows_x, full_gate, (((1,), (1,)), ((), ())), preferred_element_type=jnp.float32
    )
    pre_b = lax.dot_general(
        rows_x, full_up, (((1,), (1,)), ((), ())), preferred_element_type=jnp.float32
    )
    sig = jax.nn.sigmoid(pre_a)
    silu = pre_a * sig
    hidden = (silu * pre_b).astype(jnp.bfloat16)
    weight = recv_gate.astype(jnp.float32)
    probe = lax.dot_general(
        rows_dy, full_down, (((1,), (1,)), ((), ())), preferred_element_type=jnp.float32
    )
    share = jnp.sum(hidden.astype(jnp.float32) * probe, axis=1)
    scaled = (weight[:, None] * rows_dy.astype(jnp.float32)).astype(jnp.bfloat16)
    d_b = (weight[:, None] * probe * silu).astype(jnp.bfloat16)
    part_up = lax.dot_general(
        d_b, rows_x, (((0,), (0,)), ((), ())), preferred_element_type=jnp.float32
    )
    part_down = lax.dot_general(
        hidden, scaled, (((0,), (0,)), ((), ())), preferred_element_type=jnp.float32
    )
    folded = share.reshape(SPLIT, rows_all)
    for bit in reversed(range(levels)):
        half = folded.shape[0] // 2
        lower_half = folded[:half]
        upper_half = folded[half:]
        lower = here // (1 << bit) % 2 == 0
        keep = jnp.where(lower, lower_half, upper_half)
        away = jnp.where(lower, upper_half, lower_half)
        folded = keep + partner(away, "expert", bit)
    summed = lax.all_to_all(
        folded.reshape(rows_all), "expert", split_axis=0, concat_axis=0, tiled=True
    )
    gate_grad = jnp.dot(placed_f.T, summed, precision=lax.Precision.HIGHEST)
    sum_up, sum_down = (
        lax.psum_scatter(
            part_up.astype(jnp.bfloat16), "dp", scatter_dimension=1, tiled=True
        ).astype(jnp.float32),
        lax.psum_scatter(
            part_down.astype(jnp.bfloat16), "dp", scatter_dimension=1, tiled=True
        ).astype(jnp.float32),
    )
    return (
        sum_up.astype(jnp.bfloat16),
        sum_down.astype(jnp.bfloat16),
        gate_grad.reshape(tok_count, TOP),
    )


def solution(mesh):
    in_specs = (
        P(("expert", "dp"), None),
        P(("expert", "dp"), None),
        P(("expert", "dp"), None),
        P(("expert", "dp"), None),
        P("expert", "dp"),
        P("expert", "dp"),
        P("expert", "dp"),
    )
    out_specs = (P("expert", "dp"), P("expert", "dp"), P(("expert", "dp"), None))
    return jax.shard_map(shards, mesh=mesh, in_specs=in_specs, out_specs=out_specs, check_vma=False)
```

time: 122 us -> 114 us (0.934)
  the two profiles are of different devices: /device:TPU:0 before, /device:TPU:8 now
where the time goes in v1:
time: 114 us
  Pallas kernels  106 us (93%)
  local copies, waits for them, and re-layouts  3.78 us (3%)
  other arithmetic  3.55 us (3%)
    pallas_call x1, Pallas kernels, fused(): pl.pallas_call(lambda *refs: fused_kernel(cap, *refs), out_shape=(jax.Sha...  106 us
    unnamed x8, local copies, waits for them, and re-layouts  3.78 us

profile of v1, /device:TPU:8, one launch (start us, length us, event | category | flops | bytes accessed | tf_op | source)
XLA Modules:
  0.0 113.7 jit_solution(15705896611583467655)
XLA Ops:
  0.7 0.0 copy-start.1
  0.7 0.6 copy-done.1
  1.3 0.1 fusion
  1.4 0.2 reduce_window_sum.11
  1.6 0.0 copy-start.2
  1.6 0.2 select_reduce_fusion.1
  1.8 0.5 copy-done.2
  2.3 0.7 fusion.1.refs_1_
  3.0 0.7 fusion.2.refs_0_
  3.7 105.7 %shard_map.94 = (bf16[256,896]{1,0:T(8,128)(2,1)}, bf16[256,896]{1,0:T(8,128)(2,1)}, f32[4,640]{1,0:T(4,128)}) custom-call(bf16[160,128]{1,0:T(8,128)(2,1)} %fusion.2.refs_0_, bf16[160,128]{1,0:T(8,128)(2,1)} %fusion.1.refs_1_, bf16[128,3584]{1,0:T(8,128)(2,1)} %refs_2_.1, bf16[128,3584]{1,0:T(8,128)(2,1)} %refs_3_.1, bf16[256,896]{1,0:T(8,128)(2,1)} %refs_4_.1, ...), custom_call_target="tpu_custom_call" | custom-call | tf_op jit(solution)/shard_map/pallas_call | solution.py:302
  109.4 0.9 fusion.4
  110.3 0.1 pad_maximum_fusion
  110.4 0.1 select_reduce_fusion
  110.6 0.5 bitcast_divide_fusion
  111.1 0.0 copy-start
  111.1 1.9 %copy.12 = bf16[256,896]{1,0:T(8,128)(2,1)} copy(bf16[256,896]{1,0:T(8,128)(2,1)} %get-tuple-element.16) | data formatting | bytes 917504
  113.0 0.0 copy-done
  113.0 0.8 copy.13
  (1 shorter events, 0.0 us)
Async XLA Ops:
  0.7 0.7 copy-start.1
  1.6 0.7 copy-start.2
  111.1 1.9 %copy-start = (bf16[256,896]{1,0:T(8,128)(2,1)S(1)}, bf16[256,896]{1,0:T(8,128)(2,1)}, u32[]{:S(2)}) copy-start(bf16[256,896]{1,0:T(8,128)(2,1)} %get-tuple-element.17) | copy-start | bytes 1376260

commit v2 on v1

--- a/solution.py
+++ b/solution.py
@@ -9,7 +9,7 @@
 TOP = 1
 TOK_DEV = 128
 MESH = pl.DeviceIdType.MESH
-ORDER = (0, 4, 1, 5)
+ORDER = (0, 1, 4, 5)
 PLACE = {c: i for i, c in enumerate(ORDER)}
 PIECE = 256
 
@@ -24,15 +24,16 @@
 def fused_kernel(
     cap, oh_ref, ohg_ref, tok_ref, cot_ref, wg_ref, wu_ref, wd_ref,
     up_ref, down_ref, share_ref,
-    rows_x, rows_c, near, far, w_all, t_sum, core_out, core_in, x_out, x_in, t_h, t_d,
+    rows_x, rows_c, near, far, relay, w_all, t_sum, core_out, core_in, x_out, x_in, t_h, t_d,
     own, z_out, z_in, share_mine, share_all,
-    local_sem, row_send, row_recv, w_send, w_recv, core_send, core_recv, x_send, x_recv,
+    local_sem, row_send, row_recv, far_send, far_recv, w_send, w_recv, core_send, core_recv, x_send, x_recv,
     act_send, act_recv, z_send, z_recv, share_send, share_recv,
 ):
     e = lax.axis_index("expert")
     d = lax.axis_index("dp")
     hidden, cols = wg_ref.shape
     half = t_sum.shape[2]
+    PARTS = ((0, 256), (256, half), (0, half))
     per = hidden // PIECE
     nt = (((1,), (1,)), ((), ()))
     nn = (((1,), (0,)), ((), ()))
@@ -44,20 +45,24 @@
         return {"expert": flip(e, code), "dp": flip(d, rel)}
 
     barrier = pltpu.get_barrier_semaphore()
-    peers = ((0, 1), (0, 2), (0, 3), (1, 0), (2, 0), (4, 0), (4, 1), (4, 2), (4, 3), (5, 0))
+    peers = ((0, 1), (0, 2), (0, 3), (1, 0), (2, 0), (4, 0), (5, 0))
     for code, rel in peers:
         pl.semaphore_signal(barrier, inc=1, device_id=at_device(code, rel), device_id_type=MESH)
     pl.semaphore_wait(barrier, len(peers))
 
     sent = []
 
-    def push(src, dst, send_sem, recv_sem, device):
+    def plan(src, dst, send_sem, recv_sem, device):
         copy = pltpu.make_async_remote_copy(
             src_ref=src, dst_ref=dst, send_sem=send_sem, recv_sem=recv_sem,
             device_id=device, device_id_type=MESH,
         )
+        sent.append(copy)
+        return copy
+
+    def push(*what):
+        copy = plan(*what)
         copy.start()
-        sent.append(copy)
         return copy
 
     rows = (rows_x, rows_c)
@@ -65,7 +70,7 @@
     hots = (oh_ref, ohg_ref)
 
     def block(kind, rel, source_x, code):
-        number = (rel % 2) * 8 + source_x * 4 + PLACE[code]
+        number = (rel % 2) * 8 + PLACE[code] * 2 + source_x
         return rows[kind].at[pl.ds(pl.multiple_of(number * cap, 16), cap), :]
 
     def pick(kind, low, rel):
@@ -81,15 +86,27 @@
             source, there, row_send.at[kind, PLACE[code], rel], row_recv.at[kind, PLACE[code], rel], device
         )
 
+    far_copy = {}
+
     def send_far(kind, rel):
         far[kind, rel] = pick(kind, cap, rel)
-        send_block(kind, 4, rel, far.at[kind, rel], block(kind, rel, x_here, 4), x_here, at_device(4, rel))
+        if rel:
+            far_copy[kind, rel] = push(
+                far.at[kind, rel], relay.at[kind, rel - 1],
+                far_send.at[kind, rel], far_recv.at[kind, rel], at_device(0, rel),
+            )
+
+    def go_far(kind, rel):
+        if rel:
+            far_copy[kind, rel].wait_recv()
+        source = relay.at[kind, rel - 1] if rel else far.at[kind, 0]
+        source_x = x_there if rel // 2 else x_here
+        send_block(kind, 4, rel, source, block(kind, rel, source_x, 4), source_x, at_device(4, 0))
 
     def send_near(kind, rel):
         if rel == 0:
             mine = block(kind, 0, x_here, 0)
             mine[...] = pick(kind, 0, 0)
-            pass_on(kind, 0, 0)
         else:
             near[kind, rel - 1] = pick(kind, 0, rel)
             send_block(
@@ -114,10 +131,15 @@
     w_copy = {}
     local = {}
 
-    def w_own(k):
-        w_copy[k] = push(
+    for k in (0, 1, 2):
+        w_copy[k] = plan(
             w_in[k], w_all.at[k, hidden : 2 * hidden], w_send.at[k], w_recv.at[k], at_device(2, 0)
         )
+
+    def w_own(k, core):
+        @pl.when(d % 2 == core)
+        def _():
+            w_copy[k].start()
 
     def w_keep(k):
         local[k] = pltpu.make_async_copy(w_in[k], w_all.at[k, 0:hidden], local_sem.at[k])
@@ -131,28 +153,35 @@
     act_copy = {}
     z_copy = {}
 
-    def project(k, q):
-        out = lax.dot_general(
-            w_all[k, span(q), :], rows[k // 2][...], nt, preferred_element_type=f32
-        )
-        core_out[k, span(q), :] = out[:, half:]
-        core_copy[k, q] = push(
-            core_out.at[k, span(q)], core_in.at[k, span(q)],
-            core_send.at[k, q], core_recv.at[k, q], at_device(0, 1),
-        )
-        t_sum[k, span(q), :] = out[:, :half]
-
-    def cross(k, q):
-        core_copy[k, q].wait_recv()
-        both = t_sum[k, span(q), :] + core_in[k, span(q), :]
-        x_out[k, span(q), :] = both.astype(bf16)
-        x_copy[k, q] = push(
-            x_out.at[k, span(q)], x_in.at[k, span(q)], x_send.at[k, q], x_recv.at[k, q], at_device(0, 2)
-        )
-        t_sum[k, span(q), :] = both
+    def project(k, q, part):
+        low, high = PARTS[part]
+        weight = w_all[k, span(q), :]
+        core_out[k, span(q), low:high] = lax.dot_general(
+            weight, rows[k // 2][half + low : half + high, :], nt, preferred_element_type=f32
+        )
+        core_copy[k, q, part] = push(
+            core_out.at[k, span(q), low:high], core_in.at[k, span(q), low:high],
+            core_send.at[k, q, part], core_recv.at[k, q, part], at_device(0, 1),
+        )
+        t_sum[k, span(q), low:high] = lax.dot_general(
+            weight, rows[k // 2][low:high, :], nt, preferred_element_type=f32
+        )
+
+    def cross(k, q, part):
+        low, high = PARTS[part]
+        core_copy[k, q, part].wait_recv()
+        both = t_sum[k, span(q), low:high] + core_in[k, span(q), low:high]
+        x_out[k, span(q), low:high] = both.astype(bf16)
+        x_copy[k, q, part] = push(
+            x_out.at[k, span(q), low:high], x_in.at[k, span(q), low:high],
+            x_send.at[k, q, part], x_recv.at[k, q, part], at_device(0, 2),
+        )
+        t_sum[k, span(q), low:high] = both
 
     def total(k, q):
-        x_copy[k, q].wait_recv()
+        for part in (0, 1, 2):
+            if (k, q, part) in x_copy:
+                x_copy[k, q, part].wait_recv()
         return t_sum[k, span(q), :] + x_in[k, span(q), :].astype(f32)
 
     def hand_over(g, ref, q):
@@ -194,62 +223,89 @@
     mine_q = tuple(range(per))
     their_q = tuple(range(per, 2 * per))
 
-    for rel in (2, 0, 3, 1):
+    def do_project(k, qs, part):
+        for q in qs:
+            project(k, q, part)
+
+    def do_cross(k, qs, part):
+        for q in qs:
+            cross(k, q, part)
+
+    def all_got(kind, code):
+        for rel in (0, 1, 2, 3):
+            got(kind, code, rel)
+
+    for rel in (2, 3, 1, 0):
         send_far(0, rel)
-    for rel in (0, 2, 3, 1):
+    w_own(0, 1)
+    go_far(0, 0)
+    send_near(0, 0)
+    pass_on(0, 0, 0)
+    for rel in (2, 3, 1):
         send_near(0, rel)
-    for k in (0, 1):
-        w_own(k)
+    go_far(0, 1)
+    for rel in (2, 3, 1, 0):
+        send_far(1, rel)
+    forward(0, 0, 1)
+    for rel in (2, 3, 1, 0):
+        send_near(1, rel)
     for k in (0, 1, 2):
         w_keep(k)
-    for rel in (2, 0, 3, 1):
-        send_far(1, rel)
-    for rel in (2, 3, 1):
-        send_near(1, rel)
-    w_own(2)
-    for rel in (1, 2, 3):
-        forward(0, 0, rel)
-    for rel in (0, 1, 2, 3):
-        forward(0, 4, rel)
-    send_near(1, 0)
-    for rel in (1, 2, 3):
-        forward(1, 0, rel)
-    for code in (1, 5):
-        for rel in (0, 1, 2, 3):
-            got(0, code, rel)
-    for k in (0, 1):
-        local[k].wait()
-        for q in mine_q:
-            project(k, q)
-    for k in (0, 1):
-        for q in mine_q:
-            cross(k, q)
-    for rel in (0, 1):
-        forward(1, 4, rel)
-    for k in (0, 1):
-        w_copy[k].wait_recv()
-        for q in their_q:
-            project(k, q)
-    for k in (0, 1):
-        for q in their_q:
-            cross(k, q)
-    for rel in (2, 3):
-        forward(1, 4, rel)
+    go_far(0, 2)
+    go_far(0, 3)
+    w_own(0, 0)
+    w_own(1, 1)
+    go_far(1, 0)
+    go_far(1, 1)
+    forward(0, 4, 0)
+    forward(0, 0, 2)
+    forward(0, 0, 3)
+    forward(0, 4, 1)
+    pass_on(1, 0, 0)
+    go_far(1, 2)
+    go_far(1, 3)
+    w_own(1, 0)
+    w_own(2, 0)
+    w_own(2, 1)
+    all_got(0, 1)
+    local[0].wait()
+    do_project(0, mine_q, 0)
+    local[1].wait()
+    do_project(1, mine_q, 0)
+    do_cross(0, mine_q, 0)
+    do_cross(1, mine_q, 0)
+    forward(0, 4, 2)
+    forward(1, 0, 1)
+    w_copy[0].wait_recv()
+    do_project(0, their_q, 0)
+    do_cross(0, their_q, 0)
+    forward(0, 4, 3)
+    forward(1, 0, 2)
+    forward(1, 0, 3)
+    all_got(0, 5)
+    do_project(0, mine_q, 1)
+    do_project(1, mine_q, 1)
+    do_cross(0, mine_q, 1)
+    do_cross(1, mine_q, 1)
+    forward(1, 4, 0)
+    do_project(0, their_q, 1)
+    do_cross(0, their_q, 1)
+    forward(1, 4, 1)
+    w_copy[1].wait_recv()
+    do_project(1, their_q, 2)
+    do_cross(1, their_q, 2)
+    forward(1, 4, 2)
     for q in mine_q:
         activate(q)
-    for code in (1, 5):
-        for rel in (0, 1, 2, 3):
-            got(1, code, rel)
+    forward(1, 4, 3)
+    all_got(1, 1)
+    all_got(1, 5)
     w_copy[2].wait_recv()
-    for q in their_q:
-        project(2, q)
+    do_project(2, their_q, 2)
+    do_cross(2, their_q, 2)
     local[2].wait()
-    for q in their_q:
-        cross(2, q)
-    for q in mine_q:
-        project(2, q)
-    for q in mine_q:
-        cross(2, q)
+    do_project(2, mine_q, 2)
+    do_cross(2, mine_q, 2)
     for q in their_q:
         activate(q)
     for q in their_q:
@@ -313,6 +369,7 @@
             pltpu.VMEM((2 * half, cols), bf16),
             pltpu.VMEM((2, 3, cap, cols), bf16),
             pltpu.VMEM((2, 4, cap, cols), bf16),
+            pltpu.VMEM((2, 3, cap, cols), bf16),
             pltpu.VMEM((3, 2 * hidden, cols), bf16),
             pltpu.VMEM((3, 2 * hidden, half), f32),
             pltpu.VMEM((3, 2 * hidden, half), f32),
@@ -328,9 +385,10 @@
             pltpu.VMEM((4, 8, half), f32),
             dma((3,)),
             dma((2, 4, 4)), dma((2, 4, 4)),
+            dma((2, 4)), dma((2, 4)),
             dma((3,)), dma((3,)),
-            dma((3, 2 * per)), dma((3, 2 * per)),
-            dma((3, 2 * per)), dma((3, 2 * per)),
+            dma((3, 2 * per, 3)), dma((3, 2 * per, 3)),
+            dma((3, 2 * per, 3)), dma((3, 2 * per, 3)),
             dma((2, 2 * per)), dma((2, 2 * per)),
             dma((2, per)), dma((2, per)),
             dma((4,)), dma((4,)),
@@ -339,11 +397,11 @@
             collective_id=0, has_side_effects=True, vmem_limit_bytes=60 * 1024 * 1024
         ),
     )(hot, hot_gate, tokens, cotangent, w_gate, w_up, w_down)
-    count = len(ORDER) * cap
-    share = lax.dynamic_slice_in_dim(share, lax.axis_index("dp") // 2 * count, count, 1)
+    share = share.reshape(4, 4, 2, cap)
+    share = lax.dynamic_index_in_dim(share, lax.axis_index("dp") // 2, 2, False)
     sums = []
     for codes in ((0, 1), (4, 5)):
-        sums.append(sum(share[PLACE[c], PLACE[c] * cap : (PLACE[c] + 1) * cap] for c in codes))
+        sums.append(sum(share[PLACE[c], PLACE[c]] for c in codes))
     summed = jnp.concatenate(sums)
     gate_grad = jnp.sum(jnp.where(placed, summed[:, None], 0.0), axis=0)
     gate_grad = gate_grad / weight.astype(f32)

time: 114 us -> 107 us (0.939)
  the two profiles are of different devices: /device:TPU:8 before, /device:TPU:0 now
where the time goes in v2:
time: 107 us; the launch traced here: 106 us
  Pallas kernels  98.2 us (92%)
  local copies, waits for them, and re-layouts  4.76 us (4%)
  other arithmetic  2.64 us (2%)
    pallas_call x1, Pallas kernels, fused(): pl.pallas_call(lambda *refs: fused_kernel(cap, *refs), out_shape=(jax.Sha...  98.2 us
    unnamed x8, local copies, waits for them, and re-layouts  3.95 us

profile of v2, /device:TPU:0, one launch (start us, length us, event | category | flops | bytes accessed | tf_op | source)
XLA Modules:
  0.0 106.3 jit_solution(14838234371151175855)
XLA Ops:
  0.7 0.0 copy-start.1
  0.7 0.6 copy-done.1
  1.3 0.1 fusion
  1.4 0.2 reduce_window_sum.11
  1.6 0.2 select_reduce_fusion.1
  1.8 0.0 copy-start.2
  1.8 0.7 copy-done.2
  2.4 0.7 fusion.1.refs_1_
  3.1 0.7 fusion.2.refs_0_
  3.9 98.2 %shard_map.94 = (bf16[256,896]{1,0:T(8,128)(2,1)}, bf16[256,896]{1,0:T(8,128)(2,1)}, f32[4,640]{1,0:T(4,128)}) custom-call(bf16[160,128]{1,0:T(8,128)(2,1)} %fusion.2.refs_0_, bf16[160,128]{1,0:T(8,128)(2,1)} %fusion.1.refs_1_, bf16[128,3584]{1,0:T(8,128)(2,1)} %refs_2_.1, bf16[128,3584]{1,0:T(8,128)(2,1)} %refs_3_.1, bf16[256,896]{1,0:T(8,128)(2,1)} %refs_4_.1, ...), custom_call_target="tpu_custom_call" | custom-call | tf_op jit(solution)/shard_map/pallas_call | solution.py:358
  102.1 0.8 reshape.32
  102.9 0.1 pad_maximum_fusion
  103.0 0.1 select_reduce_fusion
  103.1 0.5 bitcast_divide_fusion
  103.7 0.0 copy-start
  103.7 1.9 %copy.12 = bf16[256,896]{1,0:T(8,128)(2,1)} copy(bf16[256,896]{1,0:T(8,128)(2,1)} %get-tuple-element.16) | data formatting | bytes 917504
  105.5 0.0 copy-done
  105.5 0.8 copy.13
  (3 shorter events, 0.0 us)
Async XLA Ops:
  0.7 0.7 copy-start.1
  1.8 0.7 copy-start.2
  103.7 1.9 %copy-start = (bf16[256,896]{1,0:T(8,128)(2,1)S(1)}, bf16[256,896]{1,0:T(8,128)(2,1)}, u32[]{:S(2)}) copy-start(bf16[256,896]{1,0:T(8,128)(2,1)} %get-tuple-element.17) | copy-start | bytes 1376260

commit v3 on v2

--- a/solution.py
+++ b/solution.py
@@ -249,6 +249,7 @@
     forward(0, 0, 1)
     for rel in (2, 3, 1, 0):
         send_near(1, rel)
+    pass_on(1, 0, 0)
     for k in (0, 1, 2):
         w_keep(k)
     go_far(0, 2)
@@ -261,7 +262,6 @@
     forward(0, 0, 2)
     forward(0, 0, 3)
     forward(0, 4, 1)
-    pass_on(1, 0, 0)
     go_far(1, 2)
     go_far(1, 3)
     w_own(1, 0)
@@ -284,32 +284,32 @@
     forward(1, 0, 3)
     all_got(0, 5)
     do_project(0, mine_q, 1)
-    do_project(1, mine_q, 1)
     do_cross(0, mine_q, 1)
-    do_cross(1, mine_q, 1)
-    forward(1, 4, 0)
     do_project(0, their_q, 1)
     do_cross(0, their_q, 1)
+    forward(1, 4, 0)
+    do_project(1, mine_q, 1)
     forward(1, 4, 1)
     w_copy[1].wait_recv()
     do_project(1, their_q, 2)
     do_cross(1, their_q, 2)
+    do_cross(1, mine_q, 1)
     forward(1, 4, 2)
+    forward(1, 4, 3)
+    all_got(1, 1)
+    w_copy[2].wait_recv()
+    all_got(1, 5)
+    do_project(2, their_q, 2)
+    do_cross(2, their_q, 2)
+    for q in their_q:
+        activate(q)
+    local[2].wait()
+    do_project(2, mine_q, 2)
+    for q in their_q:
+        gradient(1, q)
+    do_cross(2, mine_q, 2)
     for q in mine_q:
         activate(q)
-    forward(1, 4, 3)
-    all_got(1, 1)
-    all_got(1, 5)
-    w_copy[2].wait_recv()
-    do_project(2, their_q, 2)
-    do_cross(2, their_q, 2)
-    local[2].wait()
-    do_project(2, mine_q, 2)
-    do_cross(2, mine_q, 2)
-    for q in their_q:
-        activate(q)
-    for q in their_q:
-        gradient(1, q)
     for q in mine_q:
         gradient(1, q)
     for q in their_q:

time: 107 us -> 103 us (0.963)
  Pallas kernels: 98.2 us -> 94.3 us
    pallas_call x1, Pallas kernels: 98.2 us -> 94.3 us  [fused(): pl.pallas_call(lambda *refs: fused_kernel(cap, *refs), out_shape=(jax.Sha...]
where the time goes in v3:
time: 103 us; the launch traced here: 102 us
  Pallas kernels  94.3 us (92%)
  local copies, waits for them, and re-layouts  4.76 us (5%)
  other arithmetic  2.64 us (3%)
    pallas_call x1, Pallas kernels, fused(): pl.pallas_call(lambda *refs: fused_kernel(cap, *refs), out_shape=(jax.Sha...  94.3 us
    unnamed x8, local copies, waits for them, and re-layouts  3.95 us

profile of v3, /device:TPU:0, one launch (start us, length us, event | category | flops | bytes accessed | tf_op | source)
XLA Modules:
  0.0 102.4 jit_solution(1527443799027719124)
XLA Ops:
  0.7 0.0 copy-start.1
  0.7 0.6 copy-done.1
  1.3 0.1 fusion
  1.4 0.2 reduce_window_sum.11
  1.6 0.2 select_reduce_fusion.1
  1.8 0.0 copy-start.2
  1.8 0.7 copy-done.2
  2.4 0.7 fusion.1.refs_1_
  3.1 0.7 fusion.2.refs_0_
  3.9 94.3 %shard_map.94 = (bf16[256,896]{1,0:T(8,128)(2,1)}, bf16[256,896]{1,0:T(8,128)(2,1)}, f32[4,640]{1,0:T(4,128)}) custom-call(bf16[160,128]{1,0:T(8,128)(2,1)} %fusion.2.refs_0_, bf16[160,128]{1,0:T(8,128)(2,1)} %fusion.1.refs_1_, bf16[128,3584]{1,0:T(8,128)(2,1)} %refs_2_.1, bf16[128,3584]{1,0:T(8,128)(2,1)} %refs_3_.1, bf16[256,896]{1,0:T(8,128)(2,1)} %refs_4_.1, ...), custom_call_target="tpu_custom_call" | custom-call | tf_op jit(solution)/shard_map/pallas_call | solution.py:358
  98.2 0.8 reshape.32
  99.0 0.1 pad_maximum_fusion
  99.1 0.1 select_reduce_fusion
  99.2 0.5 bitcast_divide_fusion
  99.8 0.0 copy-start
  99.8 1.9 %copy.12 = bf16[256,896]{1,0:T(8,128)(2,1)} copy(bf16[256,896]{1,0:T(8,128)(2,1)} %get-tuple-element.16) | data formatting | bytes 917504
  101.6 0.0 copy-done
  101.6 0.8 copy.13
  (3 shorter events, 0.0 us)
Async XLA Ops:
  0.7 0.7 copy-start.1
  1.8 0.7 copy-start.2
  99.8 1.9 %copy-start = (bf16[256,896]{1,0:T(8,128)(2,1)S(1)}, bf16[256,896]{1,0:T(8,128)(2,1)}, u32[]{:S(2)}) copy-start(bf16[256,896]{1,0:T(8,128)(2,1)} %get-tuple-element.17) | copy-start | bytes 1376260
